TPU v7x, 32 devices: a whole 2x2x4 slice. The times are simulated.
32 devices in a mesh: dp: 2 (over x), fsdp: 16 (over z, y, core).
Axes of the slice: x: 2, y: 2, z: 4, core: 2. Of those that a mesh axis runs over, the one named last changes fastest.
Arguments:
- tokens: bfloat16 [18432, 768], P(('dp', 'fsdp')), may hold values from -6 to 6
- gain_attn: bfloat16 [768], P(('dp', 'fsdp')), may hold values from 0.25 to 1.75
- w_qkv: bfloat16 [768, 2304], P(('dp', 'fsdp')), may hold values from -0.21875 to 0.21875
- w_proj: bfloat16 [768, 768], P(('dp', 'fsdp')), may hold values from -2.5 to 2.5
- gain_moe: bfloat16 [768], P(('dp', 'fsdp')), may hold values from 0.25 to 1.75
- w_router: bfloat16 [768, 8], P(('dp', 'fsdp')), may hold values from -0.15625 to 0.15625
- w_in: bfloat16 [8, 768, 3072], P('dp', 'fsdp'), may hold values from -0.21875 to 0.21875
- w_out: bfloat16 [8, 3072, 768], P('dp', 'fsdp'), may hold values from -0.875 to 0.875
- routes: int32 [18432, 2], P(('dp', 'fsdp')), may hold values from 0 to 7, as said below
- slot_ids: int32 [18432, 2], P(('dp', 'fsdp')), may hold values from 0 to 152, as said below
- cotangent: bfloat16 [18432, 768], P(('dp', 'fsdp')), may hold values from -6 to 6
Outputs:
- output: bfloat16 [18432, 768], P(('dp', 'fsdp'))
- grad_tokens: float32 [18432, 768], P(('dp', 'fsdp'))
- d_gain_attn: float32 [768], P(('dp', 'fsdp'))
- d_qkv: float32 [768, 2304], P(('dp', 'fsdp'))
- d_proj: float32 [768, 768], P(('dp', 'fsdp'))
- d_gain_moe: float32 [768], P(('dp', 'fsdp'))
- d_router: float32 [768, 8], P(('dp', 'fsdp'))
- d_in: float32 [8, 768, 3072], P('dp', 'fsdp')
- d_out: float32 [8, 3072, 768], P('dp', 'fsdp')
Inputs may be any that keep to these rules, and one draw needn't show every extreme that they name: `routes`: each row names two different experts. `slot_ids`: among the 576 patches of one device, the pairs routed to one expert hold the distinct slots 0, 1, 2, ... in some priority order; a pair beyond the 152 slots holds 152 and is dropped. On every device some expert gets more than 152 pairs.
All inputs are finite; a program needn't handle non-finite values.
Results may differ from a plain program's by a relative error of at most 0.017.
Values may be sent and summed in bfloat16 or wider, within the bound.
No kernel may reach another device: no remote copies, remote signals or barrier semaphores. Data moves between devices by JAX's collectives and lax.ppermute only.
A program may use at most 320 MiB of HBM per device.

v0:
```python
import jax
import jax.numpy as jnp
from jax import lax
from jax.sharding import PartitionSpec as P

HEADS = 12
HEAD_DIM = 64
EXPERTS = 8
SEQ = 576
CAP = 152
norm_epsilon = 1e-06


def norm_parts(values):
    centre = values - jnp.mean(values, axis=-1, keepdims=True)
    inverse = lax.rsqrt(jnp.mean(centre * centre, axis=-1, keepdims=True) + norm_epsilon)
    return (centre * inverse, inverse)


def norm_back(grad_normed, normed, inverse):
    mean_grad = jnp.mean(grad_normed, axis=-1, keepdims=True)
    mean_cross = jnp.mean(grad_normed * normed, axis=-1, keepdims=True)
    return (grad_normed - mean_grad - normed * mean_cross) * inverse


def gelu_tanh(values):
    return jax.nn.gelu(values, approximate=True)


def head_forward(operands):
    queries, keys_head, values_head = operands
    scores = jnp.einsum(
        "isd,itd->ist", queries, keys_head, preferred_element_type=jnp.float32
    ) * HEAD_DIM ** (-0.5)
    largest = jnp.max(scores, axis=-1, keepdims=True)
    powers = jnp.exp(scores - largest)
    totals = jnp.sum(powers, axis=-1, keepdims=True)
    attn_probs = (powers / totals).astype(jnp.bfloat16)
    head_out = jnp.einsum(
        "ist,itd->isd", attn_probs, values_head, preferred_element_type=jnp.float32
    )
    return (head_out.astype(jnp.bfloat16), (largest + jnp.log(totals))[..., 0])


def head_backward(operands):
    queries, keys_head, values_head, grad_head, log_total = operands
    scores = jnp.einsum(
        "isd,itd->ist", queries, keys_head, preferred_element_type=jnp.float32
    ) * HEAD_DIM ** (-0.5)
    attn_probs = jnp.exp(scores - log_total[..., None])
    grad_probs = jnp.einsum(
        "isd,itd->ist", grad_head, values_head, preferred_element_type=jnp.float32
    )
    row_terms = jnp.sum(attn_probs * grad_probs, axis=-1, keepdims=True)
    grad_scores = (attn_probs * (grad_probs - row_terms)).astype(jnp.bfloat16)
    grad_query = jnp.einsum(
        "ist,itd->isd", grad_scores, keys_head, preferred_element_type=jnp.float32
    ) * HEAD_DIM ** (-0.5)
    grad_key = jnp.einsum(
        "ist,isd->itd", grad_scores, queries, preferred_element_type=jnp.float32
    ) * HEAD_DIM ** (-0.5)
    grad_value = jnp.einsum(
        "ist,isd->itd",
        attn_probs.astype(jnp.bfloat16),
        grad_head,
        preferred_element_type=jnp.float32,
    )
    return (grad_query, grad_key, grad_value)


def expert_forward(expert_rows, w_up, w_down):
    pre_act = jnp.einsum("ecd,edf->ecf", expert_rows, w_up, preferred_element_type=jnp.float32)
    hidden = gelu_tanh(pre_act).astype(jnp.bfloat16)
    result = jnp.einsum("ecf,efd->ecd", hidden, w_down, preferred_element_type=jnp.float32).astype(
        jnp.bfloat16
    )
    return (pre_act, hidden, result)


def expert_backward(expert_rows, pre_act, hidden, grad_result, w_up, w_down):
    grad_hidden = jnp.einsum(
        "ecd,efd->ecf", grad_result, w_down, preferred_element_type=jnp.float32
    )
    ignored, pull_back = jax.vjp(gelu_tanh, pre_act)
    grad_pre = pull_back(grad_hidden)[0].astype(jnp.bfloat16)
    grad_down = jnp.einsum("ecf,ecd->efd", hidden, grad_result, preferred_element_type=jnp.float32)
    grad_up = jnp.einsum("ecd,ecf->edf", expert_rows, grad_pre, preferred_element_type=jnp.float32)
    grad_rows = jnp.einsum(
        "ecf,edf->ecd", grad_pre, w_up, preferred_element_type=jnp.float32
    ).astype(jnp.bfloat16)
    return (grad_up, grad_down, grad_rows)


def gather_dense(gain_attn, w_qkv, w_proj, gain_moe, w_router):
    return (
        lax.all_gather(gain_attn, ("dp", "fsdp"), axis=0, tiled=True),
        lax.all_gather(w_qkv, ("dp", "fsdp"), axis=0, tiled=True),
        lax.all_gather(w_proj, ("dp", "fsdp"), axis=0, tiled=True),
        lax.all_gather(gain_moe, ("dp", "fsdp"), axis=0, tiled=True),
        lax.all_gather(w_router, ("dp", "fsdp"), axis=0, tiled=True),
    )


def gather_experts(w_in, w_out):
    local_pair = (w_in, w_out)
    return (
        lax.all_gather(local_pair[0], "fsdp", axis=1, tiled=True),
        lax.all_gather(local_pair[1], "fsdp", axis=1, tiled=True),
    )


def reduce_experts(grad_up, grad_down):
    reduced = (
        lax.psum_scatter(
            grad_up.astype(jnp.bfloat16), "fsdp", scatter_dimension=1, tiled=True
        ).astype(jnp.float32),
        lax.psum_scatter(
            grad_down.astype(jnp.bfloat16), "fsdp", scatter_dimension=1, tiled=True
        ).astype(jnp.float32),
    )
    return reduced


def per_device(
    tokens, gain_attn, w_qkv, w_proj, gain_moe, w_router, w_in, w_out, routes, slot_ids, cotangent
):
    dense_full = gather_dense(gain_attn, w_qkv, w_proj, gain_moe, w_router)
    expert_weights = gather_experts(w_in, w_out)
    rows_here = tokens.shape[0]
    images = rows_here // SEQ
    residual = tokens.astype(jnp.float32)
    normed_one, inverse_one = norm_parts(residual)
    gain_one = dense_full[0].astype(jnp.float32)
    act_one = (normed_one * gain_one).astype(jnp.bfloat16)
    qkv = jnp.dot(act_one, dense_full[1], preferred_element_type=jnp.float32).astype(jnp.bfloat16)
    split_qkv = qkv.reshape(images, SEQ, 3, HEADS, HEAD_DIM).transpose(2, 3, 0, 1, 4)
    head_out, head_lse = lax.map(head_forward, (split_qkv[0], split_qkv[1], split_qkv[2]))
    attended = head_out.transpose(1, 2, 0, 3).reshape(rows_here, -1)
    resid_mid = residual + jnp.dot(attended, dense_full[2], preferred_element_type=jnp.float32)
    normed_two, inverse_two = norm_parts(resid_mid)
    gain_two = dense_full[3].astype(jnp.float32)
    act_two = (normed_two * gain_two).astype(jnp.bfloat16)
    logits = jnp.dot(act_two, dense_full[4], preferred_element_type=jnp.float32)
    router = jax.nn.softmax(logits, axis=-1)
    expert_ids = lax.broadcasted_iota(jnp.int32, (1, 1, EXPERTS), 2)
    chosen = routes[:, :, None] == expert_ids
    gate_values = jnp.sum(jnp.where(chosen, router[:, None, :], 0.0), axis=-1)
    gates_low = gate_values.astype(jnp.bfloat16)
    slot_count = EXPERTS * CAP
    columns = lax.broadcasted_iota(jnp.int32, (1, 1, slot_count), 2)
    live_pair = slot_ids < CAP
    targets = routes * CAP + slot_ids
    matches = (targets[:, :, None] == columns) & live_pair[:, :, None]
    dispatch = jnp.sum(matches.astype(jnp.bfloat16), axis=1)
    combine = jnp.sum(
        jnp.where(matches, gates_low[:, :, None], jnp.zeros((), jnp.bfloat16)), axis=1
    )
    slot_rows = (
        jnp.einsum("tx,td->xd", dispatch, act_two, preferred_element_type=jnp.float32)
        .astype(jnp.bfloat16)
        .reshape(EXPERTS, CAP, -1)
    )
    expert_rows = lax.all_to_all(slot_rows, "dp", split_axis=0, concat_axis=1, tiled=True)
    pre_act, hidden, result = expert_forward(expert_rows, expert_weights[0], expert_weights[1])
    slot_result = lax.all_to_all(result, "dp", split_axis=1, concat_axis=0, tiled=True)
    flat_result = slot_result.reshape(slot_count, -1)
    moe_sum = jnp.einsum("tx,xd->td", combine, flat_result, preferred_element_type=jnp.float32)
    output = (resid_mid + moe_sum).astype(jnp.bfloat16)
    dense_full = gather_dense(gain_attn, w_qkv, w_proj, gain_moe, w_router)
    expert_weights = gather_experts(w_in, w_out)
    grad_slots = (
        jnp.einsum("tx,td->xd", combine, cotangent, preferred_element_type=jnp.float32)
        .astype(jnp.bfloat16)
        .reshape(EXPERTS, CAP, -1)
    )
    picked = flat_result[jnp.clip(targets, 0, slot_count - 1)]
    grad_gates = jnp.where(
        live_pair,
        jnp.einsum("tkd,td->tk", picked, cotangent, preferred_element_type=jnp.float32),
        0.0,
    )
    grad_router = jnp.sum(jnp.where(chosen, grad_gates[:, :, None], 0.0), axis=1)
    grad_logits = (
        router * (grad_router - jnp.sum(router * grad_router, axis=-1, keepdims=True))
    ).astype(jnp.bfloat16)
    d_router = jnp.einsum("td,te->de", act_two, grad_logits, preferred_element_type=jnp.float32)
    grad_act_two = jnp.einsum(
        "te,de->td", grad_logits, dense_full[4], preferred_element_type=jnp.float32
    )
    grad_expert = lax.all_to_all(grad_slots, "dp", split_axis=0, concat_axis=1, tiled=True)
    grad_up, grad_down, grad_rows = expert_backward(
        expert_rows, pre_act, hidden, grad_expert, expert_weights[0], expert_weights[1]
    )
    grad_rows = lax.all_to_all(grad_rows, "dp", split_axis=1, concat_axis=0, tiled=True)
    grad_act_two = grad_act_two + jnp.einsum(
        "tx,xd->td", dispatch, grad_rows.reshape(slot_count, -1), preferred_element_type=jnp.float32
    )
    d_gain_moe = jnp.sum(grad_act_two * normed_two, axis=0)
    grad_mid = cotangent.astype(jnp.float32) + norm_back(
        grad_act_two * gain_two, normed_two, inverse_two
    )
    grad_mid_low = grad_mid.astype(jnp.bfloat16)
    d_proj = jnp.einsum("td,te->de", attended, grad_mid_low, preferred_element_type=jnp.float32)
    grad_attended = jnp.einsum(
        "te,de->td", grad_mid_low, dense_full[2], preferred_element_type=jnp.float32
    ).astype(jnp.bfloat16)
    grad_heads = grad_attended.reshape(images, SEQ, HEADS, HEAD_DIM).transpose(2, 0, 1, 3)
    grad_query, grad_key, grad_value = lax.map(
        head_backward, (split_qkv[0], split_qkv[1], split_qkv[2], grad_heads, head_lse)
    )
    grad_qkv = (
        jnp.stack([grad_query, grad_key, grad_value])
        .transpose(2, 3, 0, 1, 4)
        .reshape(rows_here, -1)
        .astype(jnp.bfloat16)
    )
    d_qkv = jnp.einsum("td,te->de", act_one, grad_qkv, preferred_element_type=jnp.float32)
    grad_act_one = jnp.einsum(
        "te,de->td", grad_qkv, dense_full[1], preferred_element_type=jnp.float32
    )
    d_gain_attn = jnp.sum(grad_act_one * normed_one, axis=0)
    grad_tokens = grad_mid + norm_back(grad_act_one * gain_one, normed_one, inverse_one)
    dense_grads = (
        lax.psum_scatter(d_gain_attn, ("dp", "fsdp"), scatter_dimension=0, tiled=True),
        lax.psum_scatter(d_qkv, ("dp", "fsdp"), scatter_dimension=0, tiled=True),
        lax.psum_scatter(d_proj, ("dp", "fsdp"), scatter_dimension=0, tiled=True),
        lax.psum_scatter(d_gain_moe, ("dp", "fsdp"), scatter_dimension=0, tiled=True),
        lax.psum_scatter(d_router, ("dp", "fsdp"), scatter_dimension=0, tiled=True),
    )
    expert_grads = reduce_experts(grad_up, grad_down)
    return (
        output,
        grad_tokens,
        dense_grads[0],
        dense_grads[1],
        dense_grads[2],
        dense_grads[3],
        dense_grads[4],
        expert_grads[0],
        expert_grads[1],
    )


def solution(mesh):
    in_specs = (
        P(("dp", "fsdp"), None),
        P(("dp", "fsdp")),
        P(("dp", "fsdp"), None),
        P(("dp", "fsdp"), None),
        P(("dp", "fsdp")),
        P(("dp", "fsdp"), None),
        P("dp", "fsdp", None),
        P("dp", "fsdp", None),
        P(("dp", "fsdp"), None),
        P(("dp", "fsdp"), None),
        P(("dp", "fsdp"), None),
    )
    out_specs = (
        P(("dp", "fsdp"), None),
        P(("dp", "fsdp"), None),
        P(("dp", "fsdp")),
        P(("dp", "fsdp"), None),
        P(("dp", "fsdp"), None),
        P(("dp", "fsdp")),
        P(("dp", "fsdp"), None),
        P("dp", "fsdp", None),
        P("dp", "fsdp", None),
    )
    return jax.shard_map(
        per_device, mesh=mesh, in_specs=in_specs, out_specs=out_specs, check_vma=False
    )
```

profile of v0, /device:TPU:0, one launch (start us, length us, event | category | flops | bytes accessed | tf_op | source)
XLA Modules:
  0.0 1001.7 jit_solution(7998535637937780949)
XLA Ops:
  10.6 42.0 %all-reduce.6 = (bf16[768]{0:T(1024)(128)(2,1)S(1)}, bf16[768]{0:T(1024)(128)(2,1)S(1)}) all-reduce(bf16[768]{0:T(1024)(128)(2,1)S(1)} %dynamic-update-slice, bf16[768]{0:T(1024)(128)(2,1)S(1)} %dynamic-update-slice.1), channel_id=1, replica_groups=mesh['dp'=2,'fsdp'=16] {'dp','fsdp'}, use_global_device_ids=true, to_apply=%add | all-reduce | flops 1536 | bytes 6144
  52.6 40.8 %all-gather = bf16[32,24,8]{1,2,0:T(8,128)(2,1)S(1)} all-gather(bf16[1,24,8]{1,2,0:T(8,128)(2,1)S(1)} %bitcast.199), channel_id=1, replica_groups=mesh['dp'=2,'fsdp'=16] {'dp','fsdp'}, dimensions={0}, use_global_device_ids=true | all-gather | bytes 12672 | tf_op jit(solution)/shard_map/all_gather | solution.py:100
  95.4 5.9 convolution_convert_fusion.3
  113.4 37.9 %while.26 = (s32[]{:T(128)}, bf16[12,1,576,64]{2,3,1,0:T(8,128)(2,1)}, f32[12,1,576]{2,1,0:T(1,128)}, bf16[12,1,576,64]{3,2,1,0:T(8,128)(2,1)S(1)}, bf16[12,1,57...) while((s32[]{:T(128)}, bf16[12,1,576,64]{2,3,1,0:T(8,128)(2,1)}, ...), condition=%wide.region_5.6_spmd, body=%wide.region_2.5_spmd.sunk | while | flops 87293376 | bytes 4531033 | solution.py:137
  171.9 18.5 %all-to-all-done.2 = bf16[8,152,768]{2,1,0:T(8,128)(2,1)S(1)} async-done(((bf16[8,152,768]{2,1,0:T(8,128)(2,1)}), bf16[8,152,768]{2,1,0:T(8,128)(2,1)S(1)}, u32[]{:S(2)}, u32[]{:S(2)}) %all-to-all-start.2) | async-done | bytes 1867808 | tf_op jit(solution)/shard_map/all_to_all | solution.py:190
  198.6 20.2 %all-to-all-done = bf16[8,152,768]{2,1,0:T(8,128)(2,1)} async-done(((bf16[8,152,768]{2,1,0:T(8,128)(2,1)}), bf16[8,152,768]{2,1,0:T(8,128)(2,1)}, u32[]{:S(2)}, u32[]{:S(2)}) %all-to-all-start) | async-done | bytes 1867808 | tf_op jit(solution)/shard_map/all_to_all | solution.py:163
  221.7 7.1 all-gather.12.cloned.1.call-done
  228.8 12.9 %fusion.77 = f32[4,304,3072]{2,1,0:T(8,128)} fusion(bf16[4,304,768]{2,1,0:T(8,128)(2,1)S(1)} %bitcast.182, bf16[4,3072,768]{2,1,0:T(8,128)(2,1)} %all-gather.12.cloned.1.call-done), kind=kOutput, calls=%fused_computation.141 | convolution fusion | flops 5737807872 | bytes 35684352 | tf_op jit(solution)/shard_map/ecd,efd->ecf/dot_general | solution.py:81
  241.7 87.4 %all-gather.10.cloned.1.call-done = bf16[4,768,3072]{2,1,0:T(8,128)(2,1)} async-done(((bf16[4,48,3072]{2,1,0:T(8,128)(2,1)}), bf16[4,768,3072]{2,1,0:T(8,128)(2,1)}) %all-gather.10.cloned.1.call-update) | async-done | bytes 18874384 | tf_op jit(solution)/shard_map/all_gather | solution.py:107
  329.1 26.9 %fusion.43 = (bf16[4,304,3072]{2,1,0:T(8,128)(2,1)}, f32[4,304,3072]{2,1,0:T(8,128)}) fusion(f32[4,304,3072]{2,1,0:T(8,128)} %fusion.77, bf16[4,304,768]{2,1,0:T(8,128)(2,1)} %bitcast.192, bf16[4,768,3072]{2,1,0:T(8,128)(2,1)} %all-gather.10.cloned.1.call-done), kind=kOutput, calls=%fused_computation.59 | convolution fusion | flops 5812518912 | bytes 58097664 | tf_op jit(solution)/shard_map/ecd,edf->ecf/dot_general | solution.py:72
  356.0 16.5 %convolution_convert_fusion.2 = bf16[4,768,3072]{2,1,0:T(8,128)(2,1)} fusion(bf16[4,304,768]{2,1,0:T(8,128)(2,1)} %bitcast.193, bf16[4,304,3072]{2,1,0:T(8,128)(2,1)} %get-tuple-element.212), kind=kOutput, calls=%fused_computation.62 | convolution fusion | flops 5747245056 | bytes 28213248 | tf_op jit(solution)/shard_map/ecd,ecf->edf/dot_general | solution.py:87
  372.8 20.0 %convolution_convert_fusion.1 = bf16[4,3072,768]{2,1,0:T(8,128)(2,1)} fusion(bf16[4,304,768]{2,1,0:T(8,128)(2,1)S(1)} %bitcast.183, f32[4,304,3072]{2,1,0:T(8,128)} %get-tuple-element.213), kind=kOutput, calls=%fused_computation.61 | convolution fusion | flops 5780865024 | bytes 35684352 | tf_op jit(solution)/shard_map/ecf,ecd->efd/dot_general | solution.py:86
  392.9 19.3 %convolution_convert_fusion.7 = bf16[4,304,768]{2,1,0:T(8,128)(2,1)S(1)} fusion(bf16[4,3072,768]{2,1,0:T(8,128)(2,1)} %all-gather.12.cloned.1.call-done, f32[4,304,3072]{2,1,0:T(8,128)} %get-tuple-element.213), kind=kOutput, calls=%fused_computation.85 | convolution fusion | flops 5772361728 | bytes 35684352 | tf_op jit(solution)/shard_map/ecf,efd->ecd/dot_general | solution.py:74
  418.4 13.2 %convolution_convert_fusion.6 = bf16[4,304,768]{2,1,0:T(8,128)(2,1)} fusion(bf16[4,304,3072]{2,1,0:T(8,128)(2,1)} %get-tuple-element.212, bf16[4,768,3072]{2,1,0:T(8,128)(2,1)} %all-gather.10.cloned.1.call-done), kind=kOutput, calls=%fused_computation.84 | convolution fusion | flops 5738741760 | bytes 28213248 | tf_op jit(solution)/shard_map/ecf,edf->ecd/dot_general | solution.py:88
  435.3 6.1 all-to-all-done.1
  449.7 20.1 %all-to-all-done.3 = bf16[4,304,768]{2,0,1:T(4,128)(2,1)} async-done(((bf16[4,304,768]{2,0,1:T(4,128)(2,1)}), bf16[4,304,768]{2,0,1:T(4,128)(2,1)}, u32[]{:S(2)}, u32[]{:S(2)}) %all-to-all-start.3) | async-done | bytes 1867808 | tf_op jit(solution)/shard_map/all_to_all | solution.py:194
  482.4 6.0 fusion.62
  503.7 100.7 %while.27 = (s32[]{:T(128)}, bf16[12,1,576,64]{2,3,1,0:T(8,128)(2,1)}, bf16[12,1,576,64]{2,3,1,0:T(8,128)(2,1)}, bf16[12,1,576,64]{2,3,1,0:T(8,128)(2,1)}, bf16[...) while((s32[]{:T(128)}, ...), condition=%wide.region_19.20_spmd, body=%wide.region_17.19_spmd.sunk | while | flops 215064000 | bytes 11510129 | solution.py:208
  608.4 5.5 fusion.71
  615.2 7.2 fusion.60
  622.4 43.2 %all-reduce.5 = (f32[768]{0:T(1024)S(1)}, f32[768]{0:T(1024)S(1)}, f32[768,8]{0,1:T(8,128)S(1)}) all-reduce(f32[768]{0:T(1024)S(1)} %get-tuple-element.158, f32[768]{0:T(1024)S(1)} %get-tuple-element.156, f32[768,8]{0,1:T(8,128)S(1)} %fusion.79), channel_id=2, replica_groups=mesh['dp'=2,'fsdp'=16] {'dp','fsdp'}, use_global_device_ids=true, to_apply=%region_23.24.clone | all-reduce | flops 7680 | bytes 61440
  676.7 88.2 %reduce-scatter.12.cloned.1.call-done = bf16[4,192,768]{2,1,0:T(8,128)(2,1)} async-done(((bf16[4,3072,768]{2,1,0:T(8,128)(2,1)}), bf16[4,192,768]{2,1,0:T(8,128)(2,1)}) %reduce-scatter.12.cloned.1.call-update) | async-done | bytes 1179664 | tf_op jit(solution)/shard_map/reduce_scatter | solution.py:117
  767.8 101.8 %reduce-scatter.8.cloned.1.call-done = f32[24,768]{1,0:T(8,128)} async-done(((f32[768,768]{1,0:T(8,128)}), f32[24,768]{1,0:T(8,128)}) %reduce-scatter.8.cloned.1.call-update) | async-done | bytes 73744 | tf_op jit(solution)/shard_map/reduce_scatter | solution.py:226
  869.6 124.8 %reduce-scatter.6.cloned.1.call-done = f32[24,2304]{1,0:T(8,128)} async-done(((f32[768,2304]{1,0:T(8,128)}), f32[24,2304]{1,0:T(8,128)}) %reduce-scatter.6.cloned.1.call-update) | async-done | bytes 221200 | tf_op jit(solution)/shard_map/reduce_scatter | solution.py:225
  (316 shorter events, 252.4 us)
Async XLA Ops:
  7.2 45.4 %copy-start.34 = (bf16[24,8]{0,1:T(8,128)(2,1)S(1)}, bf16[24,8]{0,1:T(8,128)(2,1)}, u32[]{:S(2)}) copy-start(bf16[24,8]{0,1:T(8,128)(2,1)} %param.20) | copy-start | bytes 1156
  7.2 86.3 %copy-start.8 = (bf16[576,768]{1,0:T(8,128)(2,1)S(1)}, bf16[576,768]{1,0:T(8,128)(2,1)}, u32[]{:S(2)}) copy-start(bf16[576,768]{1,0:T(8,128)(2,1)} %param.15) | copy-start | bytes 2654212
  7.2 88.2 %all-gather.6.cloned.1.call-start = ((), (), s32[]{:S(2)}) async-start(), calls=%async_computation.8 | async-start | bytes 3649536 | tf_op jit(solution)/shard_map/all_gather | solution.py:97
  8.0 143.4 %all-gather.8.cloned.1.call-start = ((), (), s32[]{:S(2)}) async-start(), calls=%async_computation.9 | async-start | bytes 1216512 | tf_op jit(solution)/shard_map/all_gather | solution.py:98
  8.7 220.1 %all-gather.12.cloned.1.call-start = ((), (), s32[]{:S(2)}) async-start(), calls=%async_computation.11 | async-start | bytes 20054016 | tf_op jit(solution)/shard_map/all_gather | solution.py:108
  9.4 84.7 %copy-start.21 = (s32[576,2]{0,1:T(2,128)S(1)}, s32[576,2]{0,1:T(2,128)}, u32[]{:S(2)}) copy-start(s32[576,2]{0,1:T(2,128)} %param.24) | copy-start | bytes 13828
  9.4 85.3 %copy-start.23 = (s32[576,2]{0,1:T(2,128)S(1)}, s32[576,2]{0,1:T(2,128)}, u32[]{:S(2)}) copy-start(s32[576,2]{0,1:T(2,128)} %param.23) | copy-start | bytes 13828
  9.5 319.6 %all-gather.10.cloned.1.call-start = ((), (), s32[]{:S(2)}) async-start(), calls=%async_computation.10 | async-start | bytes 20054016 | tf_op jit(solution)/shard_map/all_gather | solution.py:107
  52.6 42.8 %copy-start.29 = (f32[768]{0:T(1024)}, f32[768]{0:T(1024)S(1)}, u32[]{:S(2)}) copy-start(f32[768]{0:T(1024)S(1)} %convert_element_type.101) | copy-start | bytes 9220
  151.3 4.2 copy-start.5
  156.7 10.9 %copy-start.6 = (bf16[576,768]{1,0:T(8,128)(2,1)}, bf16[576,768]{1,0:T(8,128)(2,1)S(1)}, u32[]{:S(2)}) copy-start(bf16[576,768]{1,0:T(8,128)(2,1)S(1)} %multiply_convert_fusion.2) | copy-start | bytes 2654212
  156.7 4.2 copy-start.19
  163.8 26.7 %all-to-all-start.2 = ((bf16[8,152,768]{2,1,0:T(8,128)(2,1)}), bf16[8,152,768]{2,1,0:T(8,128)(2,1)S(1)}, u32[]{:S(2)}, u32[]{:S(2)}) async-start(bf16[8,152,768]{2,1,0:T(8,128)(2,1)} %bitcast.194), calls=%async_computation.2 | async-start | bytes 3735552 | tf_op jit(solution)/shard_map/all_to_all | solution.py:190
  191.7 27.1 %all-to-all-start = ((bf16[8,152,768]{2,1,0:T(8,128)(2,1)}), bf16[8,152,768]{2,1,0:T(8,128)(2,1)}, u32[]{:S(2)}, u32[]{:S(2)}) async-start(bf16[8,152,768]{2,1,0:T(8,128)(2,1)} %bitcast.191), calls=%async_computation | async-start | bytes 3735552 | tf_op jit(solution)/shard_map/all_to_all | solution.py:163
  196.5 477.2 %reduce-scatter.10.cloned.1.call-start = ((), (), s32[]{:S(2)}) async-start(), calls=%async_computation.14 | async-start | bytes 20054016 | tf_op jit(solution)/shard_map/reduce_scatter | solution.py:114
  372.6 392.4 %reduce-scatter.12.cloned.1.call-start = ((), (), s32[]{:S(2)}) async-start(), calls=%async_computation.15 | async-start | bytes 20054016 | tf_op jit(solution)/shard_map/reduce_scatter | solution.py:117
  414.4 27.0 %all-to-all-start.1 = ((bf16[4,304,768]{2,0,1:T(4,128)(2,1)}), bf16[4,304,768]{2,0,1:T(4,128)(2,1)S(1)}, u32[]{:S(2)}, u32[]{:S(2)}) async-start(bf16[4,304,768]{2,0,1:T(4,128)(2,1)} %copy.108), calls=%async_computation.1 | async-start | bytes 3735552 | tf_op jit(solution)/shard_map/all_to_all | solution.py:165
  435.3 12.2 %copy-start.28 = (s32[576,2]{0,1:T(2,128)S(1)}, s32[576,2]{0,1:T(2,128)}, u32[]{:S(2)}) copy-start(s32[576,2]{0,1:T(2,128)} %get-tuple-element.199) | copy-start | bytes 13828
  442.6 27.1 %all-to-all-start.3 = ((bf16[4,304,768]{2,0,1:T(4,128)(2,1)}), bf16[4,304,768]{2,0,1:T(4,128)(2,1)}, u32[]{:S(2)}, u32[]{:S(2)}) async-start(bf16[4,304,768]{2,0,1:T(4,128)(2,1)} %copy.112), calls=%async_computation.3 | async-start | bytes 3735552 | tf_op jit(solution)/shard_map/all_to_all | solution.py:194
  447.4 422.2 %reduce-scatter.8.cloned.1.call-start = ((), (), s32[]{:S(2)}) async-start(), calls=%async_computation.13 | async-start | bytes 2433024 | tf_op jit(solution)/shard_map/reduce_scatter | solution.py:226
  482.4 7.1 copy-start.22
  482.4 7.3 copy-start.16
  503.4 491.0 %reduce-scatter.6.cloned.1.call-start = ((), (), s32[]{:S(2)}) async-start(), calls=%async_computation.12 | async-start | bytes 7299072 | tf_op jit(solution)/shard_map/reduce_scatter | solution.py:225
  615.2 52.2 %copy-start.10 = (bf16[576,768]{1,0:T(8,128)(2,1)S(1)}, bf16[576,768]{1,0:T(8,128)(2,1)}, u32[]{:S(2)}) copy-start(bf16[576,768]{1,0:T(8,128)(2,1)} %param.15) | copy-start | bytes 2654212
  (26 other events, 53.1 us)
Sparse Core Ops, SparseCore 0:
  10.9 62.6 all-gather.5
  76.6 52.6 all-gather.7
  130.9 97.8 all-gather.11
  230.2 98.8 all-gather.9
  372.7 194.0 reduce-scatter.9
  570.7 194.1 reduce-scatter.11
  770.8 98.7 reduce-scatter.7
  875.8 118.5 reduce-scatter.5
where the time goes:
time: 1010 us; the launch traced here: 1000 us
  waiting for transfers between devices  477 us (47%)
  matrix products  276 us (27%)
  blocking collectives  126 us (12%)
  local copies, waits for them, and re-layouts  66.9 us (7%)
  other arithmetic  22.4 us (2%)
  starting transfers between devices  18.3 us (2%)
  between operations  15.1 us (1%)
    reduce_scatter x1, waiting for transfers between devices, per_device(): lax.psum_scatter(d_qkv, ('dp', 'fsdp'), scatter_dimension=0, tiled=True)  125 us
    reduce_scatter x1, waiting for transfers between devices, per_device(): lax.psum_scatter(d_proj, ('dp', 'fsdp'), scatter_dimension=0, tiled=True)  102 us
    reduce_scatter x1, waiting for transfers between devices, reduce_experts(): lax.psum_scatter(grad_down.astype(jnp.bfloat16), 'fsdp', scatter_dimensio...  88.2 us
    all_gather x1, waiting for transfers between devices, gather_experts(): lax.all_gather(local_pair[0], 'fsdp', axis=1, tiled=True)  87.4 us
    unnamed x2, blocking collectives  85.2 us
    all_gather x1, blocking collectives, gather_dense(): lax.all_gather(w_router, ('dp', 'fsdp'), axis=0, tiled=True)  40.8 us
    dot_general x1, matrix products, expert_forward(): jnp.einsum('ecd,edf->ecf', expert_rows, w_up, preferred_element_type=jnp....  26.9 us
    dot_general x12, matrix products, head_forward(): jnp.einsum('ist,itd->isd', attn_probs, values_head, preferred_element_typ...  23.4 us
  transfers between devices with their start and end apart: 12, of which 9 were waited for; matrix products, arithmetic and copies ran while one was open for 31% of the time, Pallas kernels for 0%

commit v1 on v0

--- a/solution.py
+++ b/solution.py
@@ -191,7 +191,10 @@
     grad_up, grad_down, grad_rows = expert_backward(
         expert_rows, pre_act, hidden, grad_expert, expert_weights[0], expert_weights[1]
     )
-    grad_rows = lax.all_to_all(grad_rows, "dp", split_axis=1, concat_axis=0, tiled=True)
+    grad_rows = jnp.concatenate(
+        lax.all_to_all(jnp.stack(jnp.split(grad_rows, lax.axis_size("dp"), axis=1)), "dp", 0, 0),
+        axis=0,
+    )
     grad_act_two = grad_act_two + jnp.einsum(
         "tx,xd->td", dispatch, grad_rows.reshape(slot_count, -1), preferred_element_type=jnp.float32
     )

time: 1010 us -> 1010 us (level)
    reduce_scatter x1, waiting for transfers between devices: 88.2 us -> 106 us  [reduce_experts(): lax.psum_scatter(grad_down.astype(jnp.bfloat16), 'fsdp', scatter_dimensio...]
    all_to_all x1, waiting for transfers between devices: 20.1 us -> 3.86 us  [per_device(): lax.all_to_all(jnp.stack(jnp.split(grad_rows, lax.axis_size('dp'), axis=1...]
where the time goes in v1:
time: 1010 us; the launch traced here: 1000 us
  waiting for transfers between devices  479 us (47%)
  matrix products  275 us (27%)
  blocking collectives  127 us (13%)
  local copies, waits for them, and re-layouts  63 us (6%)
  other arithmetic  23.7 us (2%)
  starting transfers between devices  18.3 us (2%)
  between operations  15.1 us (1%)
    reduce_scatter x1, waiting for transfers between devices, per_device(): lax.psum_scatter(d_qkv, ('dp', 'fsdp'), scatter_dimension=0, tiled=True)  125 us
    reduce_scatter x1, waiting for transfers between devices, reduce_experts(): lax.psum_scatter(grad_down.astype(jnp.bfloat16), 'fsdp', scatter_dimensio...  106 us
    reduce_scatter x1, waiting for transfers between devices, per_device(): lax.psum_scatter(d_proj, ('dp', 'fsdp'), scatter_dimension=0, tiled=True)  102 us
    all_gather x1, waiting for transfers between devices, gather_experts(): lax.all_gather(local_pair[0], 'fsdp', axis=1, tiled=True)  87.4 us
    unnamed x2, blocking collectives  86.2 us
    all_gather x1, blocking collectives, gather_dense(): lax.all_gather(w_router, ('dp', 'fsdp'), axis=0, tiled=True)  40.8 us
    dot_general x1, matrix products, expert_forward(): jnp.einsum('ecd,edf->ecf', expert_rows, w_up, preferred_element_type=jnp....  26.7 us
    dot_general x12, matrix products, head_forward(): jnp.einsum('ist,itd->isd', attn_probs, values_head, preferred_element_typ...  23.4 us
  transfers between devices with their start and end apart: 12, of which 9 were waited for; matrix products, arithmetic and copies ran while one was open for 31% of the time, Pallas kernels for 0%

profile of v1, /device:TPU:0, one launch (start us, length us, event | category | flops | bytes accessed | tf_op | source)
XLA Modules:
  0.0 1001.5 jit_solution(12770171559320895816)
XLA Ops:
  10.6 42.0 %all-reduce.6 = (bf16[768]{0:T(1024)(128)(2,1)S(1)}, bf16[768]{0:T(1024)(128)(2,1)S(1)}) all-reduce(bf16[768]{0:T(1024)(128)(2,1)S(1)} %dynamic-update-slice, bf16[768]{0:T(1024)(128)(2,1)S(1)} %dynamic-update-slice.1), channel_id=1, replica_groups=mesh['dp'=2,'fsdp'=16] {'dp','fsdp'}, use_global_device_ids=true, to_apply=%add | all-reduce | flops 1536 | bytes 6144
  52.6 40.8 %all-gather = bf16[32,24,8]{1,2,0:T(8,128)(2,1)S(1)} all-gather(bf16[1,24,8]{1,2,0:T(8,128)(2,1)S(1)} %bitcast.198), channel_id=1, replica_groups=mesh['dp'=2,'fsdp'=16] {'dp','fsdp'}, dimensions={0}, use_global_device_ids=true | all-gather | bytes 12672 | tf_op jit(solution)/shard_map/all_gather | solution.py:100
  95.4 5.9 convolution_convert_fusion.3
  113.3 37.9 %while.26 = (s32[]{:T(128)}, bf16[12,1,576,64]{2,3,1,0:T(8,128)(2,1)}, f32[12,1,576]{2,1,0:T(1,128)}, bf16[12,1,576,64]{3,2,1,0:T(8,128)(2,1)S(1)}, bf16[12,1,57...) while((s32[]{:T(128)}, bf16[12,1,576,64]{2,3,1,0:T(8,128)(2,1)}, ...), condition=%wide.region_5.6_spmd, body=%wide.region_2.5_spmd.sunk | while | flops 87293376 | bytes 4531033 | solution.py:137
  171.9 18.5 %all-to-all-done.2 = bf16[8,152,768]{2,1,0:T(8,128)(2,1)S(1)} async-done(((bf16[8,152,768]{2,1,0:T(8,128)(2,1)}), bf16[8,152,768]{2,1,0:T(8,128)(2,1)S(1)}, u32[]{:S(2)}, u32[]{:S(2)}) %all-to-all-start.2) | async-done | bytes 1867808 | tf_op jit(solution)/shard_map/all_to_all | solution.py:190
  198.6 20.2 %all-to-all-done = bf16[8,152,768]{2,1,0:T(8,128)(2,1)} async-done(((bf16[8,152,768]{2,1,0:T(8,128)(2,1)}), bf16[8,152,768]{2,1,0:T(8,128)(2,1)}, u32[]{:S(2)}, u32[]{:S(2)}) %all-to-all-start) | async-done | bytes 1867808 | tf_op jit(solution)/shard_map/all_to_all | solution.py:163
  221.7 7.1 all-gather.12.cloned.1.call-done
  228.8 12.9 %fusion.77 = f32[4,304,3072]{2,1,0:T(8,128)} fusion(bf16[4,304,768]{2,1,0:T(8,128)(2,1)S(1)} %bitcast.183, bf16[4,3072,768]{2,1,0:T(8,128)(2,1)} %all-gather.12.cloned.1.call-done), kind=kOutput, calls=%fused_computation.144 | convolution fusion | flops 5737807872 | bytes 35684352 | tf_op jit(solution)/shard_map/ecd,efd->ecf/dot_general | solution.py:81
  241.7 87.4 %all-gather.10.cloned.1.call-done = bf16[4,768,3072]{2,1,0:T(8,128)(2,1)} async-done(((bf16[4,48,3072]{2,1,0:T(8,128)(2,1)}), bf16[4,768,3072]{2,1,0:T(8,128)(2,1)}) %all-gather.10.cloned.1.call-update) | async-done | bytes 18874384 | tf_op jit(solution)/shard_map/all_gather | solution.py:107
  329.1 26.7 %fusion.43 = (bf16[4,304,3072]{2,1,0:T(8,128)(2,1)}, f32[4,304,3072]{2,1,0:T(8,128)}) fusion(f32[4,304,3072]{2,1,0:T(8,128)} %fusion.77, bf16[4,304,768]{2,1,0:T(8,128)(2,1)} %bitcast.191, bf16[4,768,3072]{2,1,0:T(8,128)(2,1)} %all-gather.10.cloned.1.call-done), kind=kOutput, calls=%fused_computation.59 | convolution fusion | flops 5812518912 | bytes 58097664 | tf_op jit(solution)/shard_map/ecd,edf->ecf/dot_general | solution.py:72
  355.8 16.5 %convolution_convert_fusion.2 = bf16[4,768,3072]{2,1,0:T(8,128)(2,1)} fusion(bf16[4,304,768]{2,1,0:T(8,128)(2,1)} %bitcast.192, bf16[4,304,3072]{2,1,0:T(8,128)(2,1)} %get-tuple-element.199), kind=kOutput, calls=%fused_computation.62 | convolution fusion | flops 5747245056 | bytes 28213248 | tf_op jit(solution)/shard_map/ecd,ecf->edf/dot_general | solution.py:87
  372.5 20.0 %convolution_convert_fusion.1 = bf16[4,3072,768]{2,1,0:T(8,128)(2,1)} fusion(bf16[4,304,768]{2,1,0:T(8,128)(2,1)S(1)} %bitcast.184, f32[4,304,3072]{2,1,0:T(8,128)} %get-tuple-element.200), kind=kOutput, calls=%fused_computation.61 | convolution fusion | flops 5780865024 | bytes 35684352 | tf_op jit(solution)/shard_map/ecf,ecd->efd/dot_general | solution.py:86
  393.7 18.9 %convolution_convert_fusion.7 = bf16[4,304,768]{2,1,0:T(8,128)(2,1)S(1)} fusion(bf16[4,3072,768]{2,1,0:T(8,128)(2,1)} %all-gather.12.cloned.1.call-done, f32[4,304,3072]{2,1,0:T(8,128)} %get-tuple-element.200), kind=kOutput, calls=%fused_computation.86 | convolution fusion | flops 5772361728 | bytes 35684352 | tf_op jit(solution)/shard_map/ecf,efd->ecd/dot_general | solution.py:74
  418.7 13.2 %convolution_convert_fusion.6 = bf16[4,304,768]{2,1,0:T(8,128)(2,1)} fusion(bf16[4,304,3072]{2,1,0:T(8,128)(2,1)} %get-tuple-element.199, bf16[4,768,3072]{2,1,0:T(8,128)(2,1)} %all-gather.10.cloned.1.call-done), kind=kOutput, calls=%fused_computation.85 | convolution fusion | flops 5738741760 | bytes 28213248 | tf_op jit(solution)/shard_map/ecf,edf->ecd/dot_general | solution.py:88
  434.9 6.8 all-to-all-done.1
  449.5 4.8 gather_fusion
  459.0 6.0 fusion.62
  484.0 100.3 %while.27 = (s32[]{:T(128)}, bf16[12,1,576,64]{2,3,1,0:T(8,128)(2,1)}, bf16[12,1,576,64]{2,3,1,0:T(8,128)(2,1)}, bf16[12,1,576,64]{2,3,1,0:T(8,128)(2,1)}, bf16[...) while((s32[]{:T(128)}, ...), condition=%wide.region_19.20_spmd, body=%wide.region_17.19_spmd.sunk | while | flops 215064000 | bytes 11510129 | solution.py:211
  588.9 5.8 fusion.71
  596.2 7.8 fusion.60
  604.0 44.1 %all-reduce.5 = (f32[768]{0:T(1024)S(1)}, f32[768]{0:T(1024)S(1)}, f32[768,8]{0,1:T(8,128)S(1)}) all-reduce(f32[768]{0:T(1024)S(1)} %get-tuple-element.143, f32[768]{0:T(1024)S(1)} %get-tuple-element.141, f32[768,8]{0,1:T(8,128)S(1)} %fusion.79), channel_id=2, replica_groups=mesh['dp'=2,'fsdp'=16] {'dp','fsdp'}, use_global_device_ids=true, to_apply=%region_23.24.clone | all-reduce | flops 7680 | bytes 61440
  659.2 105.6 %reduce-scatter.12.cloned.1.call-done = bf16[4,192,768]{2,1,0:T(8,128)(2,1)} async-done(((bf16[4,3072,768]{2,1,0:T(8,128)(2,1)}), bf16[4,192,768]{2,1,0:T(8,128)(2,1)}) %reduce-scatter.12.cloned.1.call-update) | async-done | bytes 1179664 | tf_op jit(solution)/shard_map/reduce_scatter | solution.py:117
  767.6 101.7 %reduce-scatter.8.cloned.1.call-done = f32[24,768]{1,0:T(8,128)} async-done(((f32[768,768]{1,0:T(8,128)}), f32[24,768]{1,0:T(8,128)}) %reduce-scatter.8.cloned.1.call-update) | async-done | bytes 73744 | tf_op jit(solution)/shard_map/reduce_scatter | solution.py:229
  869.3 125.0 %reduce-scatter.6.cloned.1.call-done = f32[24,2304]{1,0:T(8,128)} async-done(((f32[768,2304]{1,0:T(8,128)}), f32[24,2304]{1,0:T(8,128)}) %reduce-scatter.6.cloned.1.call-update) | async-done | bytes 221200 | tf_op jit(solution)/shard_map/reduce_scatter | solution.py:228
  (315 shorter events, 248.3 us)
Async XLA Ops:
  7.2 45.4 %copy-start.34 = (bf16[24,8]{0,1:T(8,128)(2,1)S(1)}, bf16[24,8]{0,1:T(8,128)(2,1)}, u32[]{:S(2)}) copy-start(bf16[24,8]{0,1:T(8,128)(2,1)} %param.20) | copy-start | bytes 1156
  7.2 86.3 %copy-start.8 = (bf16[576,768]{1,0:T(8,128)(2,1)S(1)}, bf16[576,768]{1,0:T(8,128)(2,1)}, u32[]{:S(2)}) copy-start(bf16[576,768]{1,0:T(8,128)(2,1)} %param.15) | copy-start | bytes 2654212
  7.2 88.2 %all-gather.6.cloned.1.call-start = ((), (), s32[]{:S(2)}) async-start(), calls=%async_computation.8 | async-start | bytes 3649536 | tf_op jit(solution)/shard_map/all_gather | solution.py:97
  8.0 143.3 %all-gather.8.cloned.1.call-start = ((), (), s32[]{:S(2)}) async-start(), calls=%async_computation.9 | async-start | bytes 1216512 | tf_op jit(solution)/shard_map/all_gather | solution.py:98
  8.7 220.1 %all-gather.12.cloned.1.call-start = ((), (), s32[]{:S(2)}) async-start(), calls=%async_computation.11 | async-start | bytes 20054016 | tf_op jit(solution)/shard_map/all_gather | solution.py:108
  9.4 84.7 %copy-start.21 = (s32[576,2]{0,1:T(2,128)S(1)}, s32[576,2]{0,1:T(2,128)}, u32[]{:S(2)}) copy-start(s32[576,2]{0,1:T(2,128)} %param.24) | copy-start | bytes 13828
  9.4 85.3 %copy-start.23 = (s32[576,2]{0,1:T(2,128)S(1)}, s32[576,2]{0,1:T(2,128)}, u32[]{:S(2)}) copy-start(s32[576,2]{0,1:T(2,128)} %param.23) | copy-start | bytes 13828
  9.5 319.6 %all-gather.10.cloned.1.call-start = ((), (), s32[]{:S(2)}) async-start(), calls=%async_computation.10 | async-start | bytes 20054016 | tf_op jit(solution)/shard_map/all_gather | solution.py:107
  52.6 42.8 %copy-start.29 = (f32[768]{0:T(1024)}, f32[768]{0:T(1024)S(1)}, u32[]{:S(2)}) copy-start(f32[768]{0:T(1024)S(1)} %convert_element_type.101) | copy-start | bytes 9220
  151.3 4.1 copy-start.4
  151.3 4.1 copy-start.5
  156.6 10.9 %copy-start.6 = (bf16[576,768]{1,0:T(8,128)(2,1)}, bf16[576,768]{1,0:T(8,128)(2,1)S(1)}, u32[]{:S(2)}) copy-start(bf16[576,768]{1,0:T(8,128)(2,1)S(1)} %multiply_convert_fusion.2) | copy-start | bytes 2654212
  156.6 4.2 copy-start.19
  163.7 26.7 %all-to-all-start.2 = ((bf16[8,152,768]{2,1,0:T(8,128)(2,1)}), bf16[8,152,768]{2,1,0:T(8,128)(2,1)S(1)}, u32[]{:S(2)}, u32[]{:S(2)}) async-start(bf16[8,152,768]{2,1,0:T(8,128)(2,1)} %bitcast.193), calls=%async_computation.2 | async-start | bytes 3735552 | tf_op jit(solution)/shard_map/all_to_all | solution.py:190
  191.7 27.1 %all-to-all-start = ((bf16[8,152,768]{2,1,0:T(8,128)(2,1)}), bf16[8,152,768]{2,1,0:T(8,128)(2,1)}, u32[]{:S(2)}, u32[]{:S(2)}) async-start(bf16[8,152,768]{2,1,0:T(8,128)(2,1)} %bitcast.190), calls=%async_computation | async-start | bytes 3735552 | tf_op jit(solution)/shard_map/all_to_all | solution.py:163
  196.5 459.7 %reduce-scatter.10.cloned.1.call-start = ((), (), s32[]{:S(2)}) async-start(), calls=%async_computation.14 | async-start | bytes 20054016 | tf_op jit(solution)/shard_map/reduce_scatter | solution.py:114
  372.3 392.4 %reduce-scatter.12.cloned.1.call-start = ((), (), s32[]{:S(2)}) async-start(), calls=%async_computation.15 | async-start | bytes 20054016 | tf_op jit(solution)/shard_map/reduce_scatter | solution.py:117
  414.7 27.0 %all-to-all-start.1 = ((bf16[4,304,768]{2,0,1:T(4,128)(2,1)}), bf16[4,304,768]{2,0,1:T(4,128)(2,1)S(1)}, u32[]{:S(2)}, u32[]{:S(2)}) async-start(bf16[4,304,768]{2,0,1:T(4,128)(2,1)} %copy.81), calls=%async_computation.1 | async-start | bytes 3735552 | tf_op jit(solution)/shard_map/all_to_all | solution.py:165
  443.0 27.1 %all-to-all-start.3 = ((bf16[2,4,152,768]{3,2,1,0:T(8,128)(2,1)}), bf16[2,4,152,768]{3,2,1,0:T(8,128)(2,1)}, u32[]{:S(2)}, u32[]{:S(2)}) async-start(bf16[2,4,152,768]{3,2,1,0:T(8,128)(2,1)} %pad_maximum_fusion.1), calls=%async_computation.3 | async-start | bytes 3735552 | tf_op jit(solution)/shard_map/all_to_all | solution.py:195
  447.7 421.6 %reduce-scatter.8.cloned.1.call-start = ((), (), s32[]{:S(2)}) async-start(), calls=%async_computation.13 | async-start | bytes 2433024 | tf_op jit(solution)/shard_map/reduce_scatter | solution.py:229
  459.0 7.1 copy-start.22
  459.0 11.1 %copy-start.16 = (bf16[576,1216]{1,0:T(8,128)(2,1)S(1)}, bf16[576,1216]{1,0:T(8,128)(2,1)}, u32[]{:S(2)}) copy-start(bf16[576,1216]{1,0:T(8,128)(2,1)} %get-tuple-element.147) | copy-start | bytes 4202500
  483.7 510.5 %reduce-scatter.6.cloned.1.call-start = ((), (), s32[]{:S(2)}) async-start(), calls=%async_computation.12 | async-start | bytes 7299072 | tf_op jit(solution)/shard_map/reduce_scatter | solution.py:228
  596.2 53.8 %copy-start.10 = (bf16[576,768]{1,0:T(8,128)(2,1)S(1)}, bf16[576,768]{1,0:T(8,128)(2,1)}, u32[]{:S(2)}) copy-start(bf16[576,768]{1,0:T(8,128)(2,1)} %param.15) | copy-start | bytes 2654212
  (26 other events, 50.6 us)
Sparse Core Ops, SparseCore 0:
  10.9 62.6 all-gather.5
  76.6 52.8 all-gather.7
  131.0 97.7 all-gather.11
  230.2 98.8 all-gather.9
  372.4 194.0 reduce-scatter.9
  570.5 194.1 reduce-scatter.11
  770.6 98.6 reduce-scatter.7
  875.5 118.6 reduce-scatter.5
